TPU v7x, 32 devices: a whole 2x2x4 slice. The times are simulated.
32 devices in a mesh: dp: 8 (over y, x, core), tensor: 4 (over z).
Axes of the slice: x: 2, y: 2, z: 4, core: 2. Of those that a mesh axis runs over, the one named last changes fastest.
Arguments:
- tokens: bfloat16 [5120, 2048], P('dp'), may hold values from -6 to 6
- cotangent: bfloat16 [5120, 2048], P('dp'), may hold values from -6 to 6
- token_slots: int32 [5120], replicated, may hold values from 0 to 8191, as said below
- lengths: int32 [8, 3], P('dp'), may hold values from 0 to 1024, as said below
- mixer_gain: bfloat16 [2048], replicated, may hold values from 0.5 to 1.5
- query_weight: bfloat16 [2048, 1024], P(None, 'tensor'), may hold values from -0.125 to 0.125
- key_weight: bfloat16 [2048, 1024], P(None, 'tensor'), may hold values from -0.125 to 0.125
- value_weight: bfloat16 [2048, 2048], P(None, 'tensor'), may hold values from -0.125 to 0.125
- gate_weight: bfloat16 [2048, 2048], P(None, 'tensor'), may hold values from -0.125 to 0.125
- decay_down: bfloat16 [2048, 16], replicated, may hold values from -0.125 to 0.125
- decay_up: bfloat16 [1024, 16], P('tensor'), may hold values from -1.5 to 1.5
- decay_bias: bfloat16 [1024], P('tensor'), may hold values from -3 to 5
- head_gain: bfloat16 [512], replicated, may hold values from 0.5 to 1.5
- out_weight: bfloat16 [2048, 2048], P('tensor'), may hold values from -0.125 to 0.125
- feed_gain: bfloat16 [2048], replicated, may hold values from 0.5 to 1.5
- feed_gate: bfloat16 [2048, 5632], P(None, 'tensor'), may hold values from -0.125 to 0.125
- feed_up: bfloat16 [2048, 5632], P(None, 'tensor'), may hold values from -0.125 to 0.125
- feed_down: bfloat16 [5632, 2048], P('tensor'), may hold values from -0.078125 to 0.078125
Outputs:
- layer_out: bfloat16 [5120, 2048], P('dp')
- token_grad: bfloat16 [5120, 2048], P('dp')
- grad_mixer_gain: float32 [2048], P('dp')
- grad_query: float32 [2048, 1024], P('dp', 'tensor')
- grad_key: float32 [2048, 1024], P('dp', 'tensor')
- grad_value: float32 [2048, 2048], P('dp', 'tensor')
- grad_gate: float32 [2048, 2048], P('dp', 'tensor')
- grad_decay_down: float32 [2048, 16], P('dp')
- grad_decay_up: float32 [4, 256, 16], P('tensor', 'dp')
- grad_decay_bias: float32 [4, 256], P('tensor', 'dp')
- grad_head_gain: float32 [512], P('dp')
- grad_out: float32 [4, 512, 2048], P('tensor', 'dp')
- grad_feed_gain: float32 [2048], P('dp')
- grad_feed_gate: float32 [2048, 5632], P('dp', 'tensor')
- grad_feed_up: float32 [2048, 5632], P('dp', 'tensor')
- grad_feed_down: float32 [4, 1408, 2048], P('tensor', 'dp')
Inputs may be any that keep to these rules, and one draw needn't show every extreme that they name: `token_slots`: the tokens of one sequence fill consecutive positions of one owner, starting at the sum of the lengths before it; every position below the sum of its owner's lengths receives exactly one token and no position above it; the last owner's positions are all filled; of the 640 tokens of one data device's block at most 128 go to one owner, and some owner receives exactly 128 from every block. The lengths of one owner sum to at most 1024, all lengths together to 5120; a length may be 0; some owner holds one sequence of 1024 tokens.
All inputs are finite; a program needn't handle non-finite values.
Results may differ from a plain program's by a relative error of at most 0.019.
Values may be sent and summed in bfloat16 or wider, within the bound.
A program may use at most 256 MiB of HBM per device.

v0:
```python
import jax
import jax.numpy as jnp
from jax import lax
from jax.sharding import PartitionSpec as P

SPAN = 64
OWN_CAP = 1024
epsilon = 1e-06
head_floor = 1.0
highest_precision = lax.Precision.HIGHEST


def segment_ids(lengths_row, row_count):
    boundary = jnp.cumsum(lengths_row)
    position = jnp.arange(row_count, dtype=jnp.int32)
    return jnp.sum((position[:, None] >= boundary[None, :]).astype(jnp.int32), axis=1)


def norm_rows(row_block, gain_row):
    return (
        row_block
        * lax.rsqrt(jnp.mean(row_block * row_block, axis=-1, keepdims=True) + epsilon)
        * gain_row
    )


def gla_head(query_rows, key_rows, value_rows, gate_logits, out_gate, head_gain, segments):
    row_count = query_rows.shape[0]
    key_width = query_rows.shape[1]
    value_width = value_rows.shape[1]
    blocks = row_count // SPAN
    log_decay = (jax.nn.log_sigmoid(gate_logits) / 16.0).reshape(blocks, SPAN, key_width)
    cumulative = jnp.cumsum(log_decay, axis=1)
    span_total = cumulative[:, SPAN - 1, :]
    queries = (query_rows * float(key_width) ** (-0.5)).reshape(blocks, SPAN, key_width)
    key_block = key_rows.reshape(blocks, SPAN, key_width)
    value_vectors = value_rows.reshape(blocks, SPAN, value_width)
    labels = segments.reshape(blocks, SPAN)
    before = jnp.concatenate([jnp.full((1,), -1, jnp.int32), labels[:-1, SPAN - 1]])
    state_carried_in = (labels == before[:, None]).astype(jnp.float32)
    tail_mask = (labels == labels[:, SPAN - 1 :]).astype(jnp.float32)
    position = jnp.arange(SPAN, dtype=jnp.int32)
    allowed = (position[None, :, None] >= position[None, None, :]) & (
        labels[:, :, None] == labels[:, None, :]
    )
    query_decay_scaled = queries * jnp.exp(cumulative)
    key_grown = key_block * jnp.exp(-cumulative)
    key_final = key_block * jnp.exp(span_total[:, None, :] - cumulative) * tail_mask[:, :, None]
    score_matrix = jnp.einsum(
        "nid,njd->nij", query_decay_scaled, key_grown, precision=highest_precision
    )
    score_matrix = jnp.where(allowed, score_matrix, 0.0)
    inside_span_part = jnp.einsum(
        "kgp,kpc->kgc", score_matrix, value_vectors, precision=highest_precision
    )
    updates = jnp.einsum("njd,nje->nde", key_final, value_vectors, precision=highest_precision)

    def advance(carry_state, inputs):
        update, decay_total, keep_flag = inputs
        return (keep_flag * jnp.exp(decay_total)[:, None] * carry_state + update, carry_state)

    _, state_entering_span = lax.scan(
        advance,
        jnp.zeros((key_width, value_width), jnp.float32),
        (updates, span_total, state_carried_in[:, SPAN - 1]),
    )
    cross_span_part = jnp.einsum(
        "rsm,rmh->rsh",
        query_decay_scaled * state_carried_in[:, :, None],
        state_entering_span,
        precision=highest_precision,
    )
    output = (inside_span_part + cross_span_part).reshape(row_count, value_width)
    scaling = lax.rsqrt(jnp.mean(output * output, axis=-1, keepdims=True) + head_floor)
    return output * scaling * head_gain * jax.nn.silu(out_gate)


def contract_rows(left_mat, right_mat):
    return lax.dot_general(
        left_mat, right_mat, (((0,), (0,)), ((), ())), preferred_element_type=jnp.float32
    )


def times_transposed(left_mat, right_mat):
    return lax.dot_general(
        left_mat, right_mat, (((1,), (1,)), ((), ())), preferred_element_type=jnp.float32
    )


def per_device(
    tokens,
    cotangent,
    token_slots,
    lengths,
    mixer_gain,
    query_weight,
    key_weight,
    value_weight,
    gate_weight,
    decay_down,
    decay_up,
    decay_bias,
    head_gain,
    out_weight,
    feed_gain,
    feed_gate,
    feed_up,
    feed_down,
):
    groups = lax.axis_size("dp")
    member = lax.axis_index("dp")
    local_count = tokens.shape[0]
    model_width = tokens.shape[1]
    peer_cap = OWN_CAP // groups
    my_slots = lax.dynamic_slice_in_dim(token_slots, member * local_count, local_count)
    my_owner = my_slots // OWN_CAP
    owner_ids = jnp.arange(groups, dtype=jnp.int32)
    chosen = (my_owner[:, None] == owner_ids[None, :]).astype(jnp.int32)
    rank_in = jnp.sum((jnp.cumsum(chosen, axis=0) - 1) * chosen, axis=1)
    send_pos = my_owner * peer_cap + rank_in

    def pack_rows(row_block):
        buffer_rows = (
            jnp.zeros((groups * peer_cap, model_width), row_block.dtype).at[send_pos].set(row_block)
        )
        return buffer_rows.reshape(groups, peer_cap, model_width)

    arrived = (
        lax.all_to_all(pack_rows(tokens), "dp", split_axis=0, concat_axis=0, tiled=True),
        lax.all_to_all(pack_rows(cotangent), "dp", split_axis=0, concat_axis=0, tiled=True),
    )
    every_owner = (token_slots // OWN_CAP).reshape(groups, local_count)
    is_mine = (every_owner == member).astype(jnp.int32)
    recv_rank = jnp.cumsum(is_mine, axis=1) - 1
    recv_index = jnp.where(
        is_mine > 0, owner_ids[:, None] * peer_cap + recv_rank, groups * peer_cap
    )
    slot_local = (token_slots % OWN_CAP).reshape(groups, local_count)
    slot_map = (
        jnp.full((groups * peer_cap + 1,), OWN_CAP, jnp.int32)
        .at[recv_index.reshape(-1)]
        .set(slot_local.reshape(-1))[: groups * peer_cap]
    )

    def place_rows(row_block):
        flat_block = row_block.reshape(groups * peer_cap, model_width)
        return (
            jnp.zeros((OWN_CAP + 1, model_width), row_block.dtype)
            .at[slot_map]
            .set(flat_block)[:OWN_CAP]
        )

    def unplace_rows(row_block):
        padded = jnp.concatenate([row_block, jnp.zeros((1, model_width), row_block.dtype)], axis=0)
        return padded[slot_map].reshape(groups, peer_cap, model_width)

    def take_back(returned):
        return returned.reshape(groups * peer_cap, model_width)[send_pos]

    owner_rows = place_rows(arrived[0]).astype(jnp.float32)
    upstream = place_rows(arrived[1])
    labels = segment_ids(lengths[0], OWN_CAP)
    mixed_wide, mixer_norm_back = jax.vjp(norm_rows, owner_rows, mixer_gain.astype(jnp.float32))
    normed = mixed_wide.astype(jnp.bfloat16)

    def project(weight):
        return jnp.dot(normed, weight, preferred_element_type=jnp.float32)

    queries = project(query_weight).astype(jnp.bfloat16)
    keys_low = project(key_weight).astype(jnp.bfloat16)
    value_vectors = project(value_weight).astype(jnp.bfloat16)
    gate_pre = project(gate_weight)
    latent = project(decay_down)
    decay_up_wide = decay_up.astype(jnp.float32)
    logits = lax.dot_general(
        latent, decay_up_wide, (((1,), (1,)), ((), ())), precision=highest_precision
    ) + decay_bias.astype(jnp.float32)

    def mixer(query_wide, key_wide, value_wide, logit_wide, gate_wide, gain_wide):
        return gla_head(query_wide, key_wide, value_wide, logit_wide, gate_wide, gain_wide, labels)

    gated_wide, mixer_back = jax.vjp(
        mixer,
        queries.astype(jnp.float32),
        keys_low.astype(jnp.float32),
        value_vectors.astype(jnp.float32),
        logits,
        gate_pre,
        head_gain.astype(jnp.float32),
    )
    gated_low = gated_wide.astype(jnp.bfloat16)
    mixer_partial = jnp.dot(gated_low, out_weight, preferred_element_type=jnp.float32)
    hidden = owner_rows + lax.psum(mixer_partial, "tensor")
    feed_wide, feed_norm_back = jax.vjp(norm_rows, hidden, feed_gain.astype(jnp.float32))
    feed_normed = feed_wide.astype(jnp.bfloat16)
    gate_hidden = jnp.dot(feed_normed, feed_gate, preferred_element_type=jnp.float32)
    up_hidden = jnp.dot(feed_normed, feed_up, preferred_element_type=jnp.float32)
    sigmoid_gate = jax.nn.sigmoid(gate_hidden)
    swish_gate = gate_hidden * sigmoid_gate
    active = (swish_gate * up_hidden).astype(jnp.bfloat16)
    feed_partial = jnp.dot(active, feed_down, preferred_element_type=jnp.float32)
    layer_rows = (
        hidden + lax.psum(feed_partial.astype(jnp.bfloat16), "tensor").astype(jnp.float32)
    ).astype(jnp.bfloat16)
    upstream_wide = upstream.astype(jnp.float32)
    grad_feed_down = contract_rows(active, upstream)
    d_active = times_transposed(upstream, feed_down)
    d_gate_hidden = (
        d_active * up_hidden * sigmoid_gate * (1.0 + gate_hidden * (1.0 - sigmoid_gate))
    ).astype(jnp.bfloat16)
    d_up_hidden = (d_active * swish_gate).astype(jnp.bfloat16)
    grad_feed_gate = contract_rows(feed_normed, d_gate_hidden)
    grad_feed_up = contract_rows(feed_normed, d_up_hidden)
    feed_part = times_transposed(d_gate_hidden, feed_gate) + times_transposed(d_up_hidden, feed_up)
    d_feed = lax.psum(feed_part, "tensor")
    d_hidden_norm, grad_feed_gain = feed_norm_back(d_feed)
    d_hidden = upstream_wide + d_hidden_norm
    d_mixed = d_hidden.astype(jnp.bfloat16)
    gain_term = jnp.zeros((model_width,), jnp.float32)
    grad_out = contract_rows(gated_low, d_mixed)
    d_gated = times_transposed(d_mixed, out_weight)
    d_query, d_key, d_value, d_logits, d_gate, d_head_gain = mixer_back(d_gated)
    d_query_low = d_query.astype(jnp.bfloat16)
    d_key_low = d_key.astype(jnp.bfloat16)
    d_value_low = d_value.astype(jnp.bfloat16)
    d_gate_low = d_gate.astype(jnp.bfloat16)
    grad_decay_bias = jnp.sum(d_logits, axis=0)
    grad_decay_up = lax.dot_general(
        d_logits, latent, (((0,), (0,)), ((), ())), precision=highest_precision
    )
    latent_part = jnp.dot(d_logits, decay_up_wide, precision=highest_precision)
    mixer_part = (
        times_transposed(d_query_low, query_weight)
        + times_transposed(d_key_low, key_weight)
        + times_transposed(d_value_low, value_weight)
        + times_transposed(d_gate_low, gate_weight)
    )
    summed = lax.psum((mixer_part, latent_part, d_head_gain, gain_term), "tensor")
    d_latent = summed[1]
    d_normed = summed[0] + lax.dot_general(
        d_latent,
        decay_down.astype(jnp.float32),
        (((1,), (1,)), ((), ())),
        precision=highest_precision,
    )
    grad_decay_down = lax.dot_general(
        normed.astype(jnp.float32), d_latent, (((0,), (0,)), ((), ())), precision=highest_precision
    )
    grad_query = contract_rows(normed, d_query_low)
    grad_key = contract_rows(normed, d_key_low)
    grad_value = contract_rows(normed, d_value_low)
    grad_gate = contract_rows(normed, d_gate_low)
    d_rows_norm, grad_mixer_gain = mixer_norm_back(d_normed)
    token_rows = (d_hidden + d_rows_norm).astype(jnp.bfloat16)
    shares = (
        lax.psum_scatter(grad_mixer_gain, "dp", scatter_dimension=0, tiled=True),
        lax.psum_scatter(grad_query, "dp", scatter_dimension=0, tiled=True),
        lax.psum_scatter(grad_key, "dp", scatter_dimension=0, tiled=True),
        lax.psum_scatter(grad_value, "dp", scatter_dimension=0, tiled=True),
        lax.psum_scatter(grad_gate, "dp", scatter_dimension=0, tiled=True),
        lax.psum_scatter(grad_decay_down, "dp", scatter_dimension=0, tiled=True),
        lax.psum_scatter(grad_decay_up, "dp", scatter_dimension=0, tiled=True),
        lax.psum_scatter(grad_decay_bias, "dp", scatter_dimension=0, tiled=True),
        lax.psum_scatter(summed[2], "dp", scatter_dimension=0, tiled=True),
        lax.psum_scatter(grad_out, "dp", scatter_dimension=0, tiled=True),
        lax.psum_scatter(grad_feed_gain, "dp", scatter_dimension=0, tiled=True),
        lax.psum_scatter(grad_feed_gate, "dp", scatter_dimension=0, tiled=True),
        lax.psum_scatter(grad_feed_up, "dp", scatter_dimension=0, tiled=True),
        lax.psum_scatter(grad_feed_down, "dp", scatter_dimension=0, tiled=True),
    )
    returned = (
        lax.all_to_all(unplace_rows(layer_rows), "dp", split_axis=0, concat_axis=0, tiled=True),
        lax.all_to_all(unplace_rows(token_rows), "dp", split_axis=0, concat_axis=0, tiled=True),
    )
    layer_out = take_back(returned[0])
    token_grad = take_back(returned[1])
    rank_width = decay_up.shape[1]
    return (
        layer_out,
        token_grad,
        shares[0],
        shares[1],
        shares[2],
        shares[3],
        shares[4],
        shares[5],
        shares[6].reshape(1, -1, rank_width),
        shares[7].reshape(1, -1),
        shares[8],
        shares[9].reshape(1, shares[9].shape[0], model_width),
        shares[10],
        shares[11],
        shares[12],
        shares[13].reshape(1, shares[13].shape[0], model_width),
    )


def solution(mesh):
    placed = (
        P("dp", None),
        P("dp", None),
        P(),
        P("dp", None),
        P(),
        P(None, "tensor"),
        P(None, "tensor"),
        P(None, "tensor"),
        P(None, "tensor"),
        P(),
        P("tensor", None),
        P("tensor"),
        P(),
        P("tensor", None),
        P(),
        P(None, "tensor"),
        P(None, "tensor"),
        P("tensor", None),
    )
    return jax.shard_map(
        per_device,
        mesh=mesh,
        in_specs=placed,
        out_specs=(
            P("dp", None),
            P("dp", None),
            P("dp"),
            P("dp", "tensor"),
            P("dp", "tensor"),
            P("dp", "tensor"),
            P("dp", "tensor"),
            P("dp", None),
            P("tensor", "dp", None),
            P("tensor", "dp"),
            P("dp"),
            P("tensor", "dp", None),
            P("dp"),
            P("dp", "tensor"),
            P("dp", "tensor"),
            P("tensor", "dp", None),
        ),
        check_vma=False,
    )
```

profile of v0, /device:TPU:0, one launch (start us, length us, event | category | flops | bytes accessed | tf_op | source)
XLA Modules:
  0.0 2135.5 jit_solution(18394428422442927344)
XLA Ops:
  11.7 10.5 scatter_custom_fusion.1
  22.2 5.3 all-to-all-start
  30.1 19.2 scatter_custom_fusion
  50.7 26.0 %all-to-all-done = bf16[8,128,2048]{2,1,0:T(8,128)(2,1)} async-done(((bf16[8,128,2048]{2,1,0:T(8,128)(2,1)}), bf16[8,128,2048]{2,1,0:T(8,128)(2,1)}, u32[]{:S(2)}, u32[]{:S(2)}) %all-to-all-start) | async-done | bytes 4194336 | tf_op jit(solution)/shard_map/all_to_all | solution.py:129
  76.7 10.1 scatter_custom_fusion.2
  109.0 6.7 fusion.66
  120.0 61.8 %while.36 = (s32[]{:T(128)}, f32[256,512]{1,0:T(8,128)S(1)}, f32[16,256,512]{2,1,0:T(8,128)}, f32[16,256]{1,0:T(8,128)S(1)}, f32[16,256,1]{1,2,0:T(1,128)}, /*in...) while((s32[]{:T(128)}, f32[256,512]{1,0:T(8,128)S(1)}, ...), condition=%wide.region_13.14_spmd.clone, body=%wide.region_12.13_spmd.clone.sunk | while | flops 524547 | bytes 2629268 | solution.py:62
  182.4 10.8 multiply_reduce_fusion.4
  193.3 6.9 multiply_convert_fusion.4
  201.2 5.6 fusion.85
  206.8 10.9 scatter_custom_fusion.3
  217.7 4.7 all-to-all-start.2
  222.5 49.1 %all-to-all-done.2 = bf16[8,128,2048]{2,1,0:T(8,128)(2,1)} async-done(((bf16[8,128,2048]{2,1,0:T(8,128)(2,1)}), bf16[8,128,2048]{2,1,0:T(8,128)(2,1)}, u32[]{:S(2)}, u32[]{:S(2)}) %all-to-all-start.2) | async-done | bytes 4194336 | tf_op jit(solution)/shard_map/all_to_all | solution.py:130
  271.5 10.1 scatter_custom_fusion.4
  281.6 216.3 %all-reduce.14.cloned.1.call-done = f32[1024,2048]{1,0:T(8,128)} async-done(((f32[1024,2048]{1,0:T(8,128)}), f32[1024,2048]{1,0:T(8,128)}) %all-reduce.14.cloned.1.call-update) | async-done | bytes 8388624 | tf_op jit(solution)/shard_map/psum | solution.py:193
  497.9 5.5 multiply_reduce_fusion.2
  506.7 11.9 fusion.87
  518.6 10.3 fusion.86
  528.9 15.1 multiply_convert_fusion.1
  544.0 10.2 fusion.88
  554.2 10.9 convolution_add_fusion.1
  565.2 10.9 convolution_convert_fusion
  576.2 278.9 %all-reduce.18.cloned.1.call-done = f32[1024,2048]{1,0:T(8,128)} async-done(((f32[1024,2048]{1,0:T(8,128)}), f32[1024,2048]{1,0:T(8,128)}) %all-reduce.18.cloned.1.call-update) | async-done | bytes 8388624 | tf_op jit(solution)/shard_map/psum | solution.py:215
  855.1 7.6 multiply_reduce_fusion
  862.7 148.8 %all-reduce.16.cloned.1.call-done = bf16[1024,2048]{1,0:T(8,128)(2,1)} async-done(((bf16[1024,2048]{1,0:T(8,128)(2,1)}), bf16[1024,2048]{1,0:T(8,128)(2,1)}) %all-reduce.16.cloned.1.call-update) | async-done | bytes 4194320 | tf_op jit(solution)/shard_map/psum | solution.py:203
  1011.5 12.5 fusion.6
  1024.0 6.9 multiply_reduce_fusion.3
  1037.5 9.8 fusion.57
  1049.1 9.4 fusion.34
  1058.4 5.7 fusion.92
  1068.5 78.5 %while.37 = (s32[]{:T(128)}, f32[256,512]{1,0:T(8,128)S(1)}, f32[16,256,512]{2,1,0:T(8,128)}, f32[16,256]{1,0:T(8,128)S(1)}, f32[16,256,512]{2,1,0:T(8,128)}, /*...) while((s32[]{:T(128)}, f32[256,512]{1,0:T(8,128)S(1)}, ...), condition=%wide.region_25.26_spmd.clone, body=%wide.region_23.25_spmd.clone.sunk | while | flops 786692 | bytes 3157176 | solution.py:62
  1147.0 8.5 fusion.62
  1155.6 5.9 add_convert_fusion.1
  1169.4 5.6 fusion.91
  1177.4 9.1 add_add_fusion.2
  1189.8 5.7 fusion.94
  1195.7 4.9 fusion.93
  1200.8 7.8 fusion.24
  1209.9 6.7 fusion.96
  1217.8 6.6 fusion.95
  1224.4 254.9 %all-reduce.20.cloned.1.call-done = (f32[1024,2048]{1,0:T(8,128)}, f32[1024,16]{0,1:T(8,128)}) async-done(((f32[1024,2048]{1,0:T(8,128)}, f32[1024,16]{0,1:T(8,128)}), (f32[1024,2048]{1,0:T(8,128)}, f32[1024,16]{0,1:T(8,128)})) %all-reduce.20.cloned.1.call-update) | async-done | bytes 8454160 | tf_op jit(solution)/shard_map/psum | solution.py:238
  1479.3 4.6 fusion.97
  1484.0 11.4 fusion.12
  1495.6 11.9 fusion.99
  1507.6 11.9 fusion.98
  1519.5 4.8 concatenate.10
  1524.3 11.8 gather_fusion
  1536.1 4.9 all-to-all-start.1
  1541.1 8.8 fusion.5
  1553.7 4.7 concatenate.11
  1558.4 11.6 gather_fusion.2
  1570.0 26.1 %all-to-all-done.1 = bf16[8,128,2048]{2,1,0:T(8,128)(2,1)} async-done(((bf16[8,128,2048]{2,1,0:T(8,128)(2,1)}), bf16[8,128,2048]{2,1,0:T(8,128)(2,1)}, u32[]{:S(2)}, u32[]{:S(2)}) %all-to-all-start.1) | async-done | bytes 4194336 | tf_op jit(solution)/shard_map/all_to_all | solution.py:272
  1596.1 4.7 all-to-all-start.3
  1604.9 9.7 gather_fusion.1
  1614.6 60.6 %all-reduce.7 = (f32[2048]{0:T(1024)S(1)}, f32[256]{0:T(256)S(1)}, f32[512]{0:T(512)S(1)}, f32[2048]{0:T(1024)S(1)}) all-reduce(f32[2048]{0:T(1024)S(1)} %get-tuple-element.304, f32[256]{0:T(256)S(1)} %neg.53, f32[512]{0:T(512)S(1)} %copy-done.70, f32[2048]{0:T(1024)S(1)} %copy-done.62), channel_id=2, replica_groups=mesh['dp'=8,'tensor'=4] {'dp'}, use_global_device_ids=true, to_apply=%region_32.33.clone | all-reduce | flops 4864 | bytes 38912
  1676.5 12.4 psum.48
  1689.5 9.9 gather_fusion.3
  1699.4 8.6 reduce-scatter.23.cloned.1.call-done
  1708.0 55.7 %reduce-scatter.19.cloned.1.call-done = f32[256,512]{1,0:T(8,128)} async-done(((f32[2048,512]{1,0:T(8,128)}), f32[256,512]{1,0:T(8,128)}) %reduce-scatter.19.cloned.1.call-update) | async-done | bytes 524304 | tf_op jit(solution)/shard_map/reduce_scatter | solution.py:260
  1763.7 55.1 %reduce-scatter.17.cloned.1.call-done = f32[256,512]{1,0:T(8,128)} async-done(((f32[2048,512]{1,0:T(8,128)}), f32[256,512]{1,0:T(8,128)}) %reduce-scatter.17.cloned.1.call-update) | async-done | bytes 524304 | tf_op jit(solution)/shard_map/reduce_scatter | solution.py:259
  1818.8 37.3 %reduce-scatter.21.cloned.1.call-done = f32[256,16]{0,1:T(8,128)} async-done(((f32[2048,16]{0,1:T(8,128)}), f32[256,16]{0,1:T(8,128)}) %reduce-scatter.21.cloned.1.call-update) | async-done | bytes 16400 | tf_op jit(solution)/shard_map/reduce_scatter | solution.py:261
  1856.0 90.8 %reduce-scatter.29.cloned.1.call-done = f32[176,2048]{1,0:T(8,128)} async-done(((f32[1408,2048]{1,0:T(8,128)}), f32[176,2048]{1,0:T(8,128)}) %reduce-scatter.29.cloned.1.call-update) | async-done | bytes 1441808 | tf_op jit(solution)/shard_map/reduce_scatter | solution.py:269
  1946.8 90.9 %reduce-scatter.27.cloned.1.call-done = f32[256,1408]{1,0:T(8,128)} async-done(((f32[2048,1408]{1,0:T(8,128)}), f32[256,1408]{1,0:T(8,128)}) %reduce-scatter.27.cloned.1.call-update) | async-done | bytes 1441808 | tf_op jit(solution)/shard_map/reduce_scatter | solution.py:268
  2037.7 90.8 %reduce-scatter.25.cloned.1.call-done = f32[256,1408]{1,0:T(8,128)} async-done(((f32[2048,1408]{1,0:T(8,128)}), f32[256,1408]{1,0:T(8,128)}) %reduce-scatter.25.cloned.1.call-update) | async-done | bytes 1441808 | tf_op jit(solution)/shard_map/reduce_scatter | solution.py:267
  (500 shorter events, 215.6 us)
Async XLA Ops:
  7.2 186.1 %copy-start = (bf16[2048,512]{1,0:T(8,128)(2,1)S(1)}, bf16[2048,512]{1,0:T(8,128)(2,1)}, u32[]{:S(2)}) copy-start(bf16[2048,512]{1,0:T(8,128)(2,1)} %param.30) | copy-start | bytes 6291460
  11.7 195.1 %copy-start.64 = (s32[640]{0:T(1024)}, s32[640]{0:T(1024)S(1)}, u32[]{:S(2)}) copy-start(s32[640]{0:T(1024)S(1)} %compare_select_fusion.4) | copy-start | bytes 7684
  22.2 54.5 %all-to-all-start = ((bf16[8,128,2048]{2,1,0:T(8,128)(2,1)}), bf16[8,128,2048]{2,1,0:T(8,128)(2,1)}, u32[]{:S(2)}, u32[]{:S(2)}) async-start(bf16[8,128,2048]{2,1,0:T(8,128)(2,1)} %bitcast.199), calls=%async_computation | async-start | bytes 8388608 | tf_op jit(solution)/shard_map/all_to_all | solution.py:129
  27.5 470.4 %all-reduce.14.cloned.1.call-start = ((), (), s32[]{:S(2)}) async-start(), calls=%async_computation.14 | async-start | bytes 16777216 | tf_op jit(solution)/shard_map/psum | solution.py:193
  28.0 76.0 %copy-start.41 = (s32[16,64]{1,0:T(8,128)}, s32[16,64]{1,0:T(8,128)S(1)}, u32[]{:S(2)}) copy-start(s32[16,64]{1,0:T(8,128)S(1)} %eq.92) | copy-start | bytes 12292
  28.0 62.0 %copy-start.51 = (f32[2048]{0:T(1024)}, f32[2048]{0:T(1024)S(1)}, u32[]{:S(2)}) copy-start(f32[2048]{0:T(1024)S(1)} %convert_element_type.127) | copy-start | bytes 24580
  49.7 54.3 %copy-start.55 = (pred[64,64]{1,0:T(8,128)(4,1)}, pred[64,64]{1,0:T(8,128)(4,1)S(1)}, u32[]{:S(2)}) copy-start(pred[64,64]{1,0:T(8,128)(4,1)S(1)} %iota_compare_fusion) | copy-start | bytes 12292
  49.9 59.0 %copy-start.53 = (f32[16,64]{1,0:T(8,128)}, f32[16,64]{1,0:T(8,128)S(1)}, u32[]{:S(2)}) copy-start(f32[16,64]{1,0:T(8,128)S(1)} %get-tuple-element.369) | copy-start | bytes 12292
  96.7 12.3 copy-start.12
  99.0 9.9 copy-start.15
  106.6 9.0 copy-start.19
  182.4 10.8 copy-start.43
  182.4 10.8 copy-start.72
  193.3 7.9 copy-start.74
  217.7 53.8 %all-to-all-start.2 = ((bf16[8,128,2048]{2,1,0:T(8,128)(2,1)}), bf16[8,128,2048]{2,1,0:T(8,128)(2,1)}, u32[]{:S(2)}, u32[]{:S(2)}) async-start(bf16[8,128,2048]{2,1,0:T(8,128)(2,1)} %bitcast.200), calls=%async_computation.2 | async-start | bytes 8388608 | tf_op jit(solution)/shard_map/all_to_all | solution.py:130
  222.4 632.7 %all-reduce.18.cloned.1.call-start = ((), (), s32[]{:S(2)}) async-start(), calls=%async_computation.16 | async-start | bytes 16777216 | tf_op jit(solution)/shard_map/psum | solution.py:215
  506.7 11.9 copy-start.23
  506.7 22.2 %slice-start.6 = ((s8[4227072]{0:T(1024)(128)(4,1)}), s8[4194304]{0:T(1024)(128)(4,1)S(1)}, s32[]{:S(2)}) async-start(s8[4227072]{0:T(1024)(128)(4,1)} %bitcast.191), calls=%async_computation.34 | async-start | bytes 8388608
  518.6 10.3 slice-start.7
  544.0 10.2 copy-start.80
  565.1 446.4 %all-reduce.16.cloned.1.call-start = ((), (), s32[]{:S(2)}) async-start(), calls=%async_computation.15 | async-start | bytes 8388608 | tf_op jit(solution)/shard_map/psum | solution.py:203
  576.1 903.2 %all-reduce.20.cloned.1.call-start = ((), (), s32[]{:S(2)}) async-start(), calls=%async_computation.27 | async-start | bytes 16908288 | tf_op jit(solution)/shard_map/psum | solution.py:238
  1011.5 12.5 copy-start.18
  1011.5 12.5 copy-start.30
  1024.0 7.0 copy-start.4
  1032.9 25.5 %copy-start.34 = (bf16[1024,512]{1,0:T(8,128)(2,1)}, bf16[1024,512]{1,0:T(8,128)(2,1)S(1)}, u32[]{:S(2)}) copy-start(bf16[1024,512]{1,0:T(8,128)(2,1)S(1)} %get-tuple-element.363) | copy-start | bytes 3145732
  1033.0 16.1 slice-start.2
  1034.2 13.2 copy-start.21
  1037.5 9.8 copy-start.6
  1037.5 9.8 copy-start.13
  1037.5 11.5 slice-start.3
  1068.5 78.5 %copy-start.14 = (bf16[1024,256]{1,0:T(8,128)(2,1)S(1)}, bf16[1024,256]{1,0:T(8,128)(2,1)}, u32[]{:S(2)}) copy-start(bf16[1024,256]{1,0:T(8,128)(2,1)} %copy-done.12) | copy-start | bytes 1572868
  1068.5 78.5 %copy-start.44 = (f32[16,256]{1,0:T(8,128)S(1)}, f32[16,256]{1,0:T(8,128)}, u32[]{:S(2)}) copy-start(f32[16,256]{1,0:T(8,128)} %copy-done.43) | copy-start | bytes 49156
  1068.5 78.5 %copy-start.54 = (f32[16,64]{1,0:T(8,128)S(1)}, f32[16,64]{1,0:T(8,128)}, u32[]{:S(2)}) copy-start(f32[16,64]{1,0:T(8,128)} %copy-done.53) | copy-start | bytes 12292
  1147.0 8.6 copy-start.3
  1147.0 8.6 copy-start.17
  1155.6 6.0 copy-start.11
  1155.6 6.0 copy-start.22
  1155.6 6.0 copy-start.25
  1155.6 6.0 copy-start.26
  1161.6 7.8 copy-start.39
  1164.7 10.4 copy-start.27
  1169.4 6.9 slice-start.8
  1186.5 417.0 %reduce-scatter.31.cloned.1.call-start = ((), (), s32[]{:S(2)}) async-start(), calls=%async_computation.26 | async-start | bytes 147456
  1189.8 509.6 %reduce-scatter.15.cloned.1.call-start = ((), (), s32[]{:S(2)}) async-start(), calls=%async_computation.18 | async-start | bytes 2359296 | tf_op jit(solution)/shard_map/reduce_scatter | solution.py:258
  1195.6 503.8 %reduce-scatter.13.cloned.1.call-start = ((), (), s32[]{:S(2)}) async-start(), calls=%async_computation.17 | async-start | bytes 2359296 | tf_op jit(solution)/shard_map/reduce_scatter | solution.py:257
  1200.6 507.4 %reduce-scatter.23.cloned.1.call-start = ((), (), s32[]{:S(2)}) async-start(), calls=%async_computation.22 | async-start | bytes 4718592 | tf_op jit(solution)/shard_map/reduce_scatter | solution.py:265
  1208.7 555.0 %reduce-scatter.19.cloned.1.call-start = ((), (), s32[]{:S(2)}) async-start(), calls=%async_computation.20 | async-start | bytes 4718592 | tf_op jit(solution)/shard_map/reduce_scatter | solution.py:260
  1216.6 602.2 %reduce-scatter.17.cloned.1.call-start = ((), (), s32[]{:S(2)}) async-start(), calls=%async_computation.19 | async-start | bytes 4718592 | tf_op jit(solution)/shard_map/reduce_scatter | solution.py:259
  1224.4 631.7 %reduce-scatter.21.cloned.1.call-start = ((), (), s32[]{:S(2)}) async-start(), calls=%async_computation.21 | async-start | bytes 147456 | tf_op jit(solution)/shard_map/reduce_scatter | solution.py:261
  1483.9 462.9 %reduce-scatter.29.cloned.1.call-start = ((), (), s32[]{:S(2)}) async-start(), calls=%async_computation.25 | async-start | bytes 12976128 | tf_op jit(solution)/shard_map/reduce_scatter | solution.py:269
  1495.4 542.3 %reduce-scatter.27.cloned.1.call-start = ((), (), s32[]{:S(2)}) async-start(), calls=%async_computation.24 | async-start | bytes 12976128 | tf_op jit(solution)/shard_map/reduce_scatter | solution.py:268
  1507.6 620.9 %reduce-scatter.25.cloned.1.call-start = ((), (), s32[]{:S(2)}) async-start(), calls=%async_computation.23 | async-start | bytes 12976128 | tf_op jit(solution)/shard_map/reduce_scatter | solution.py:267
  1536.1 13.8 slice-start
  1536.1 60.0 %all-to-all-start.1 = ((bf16[8,128,2048]{2,1,0:T(8,128)(2,1)}), bf16[8,128,2048]{2,1,0:T(8,128)(2,1)}, u32[]{:S(2)}, u32[]{:S(2)}) async-start(bf16[8,128,2048]{2,1,0:T(8,128)(2,1)} %bitcast.198), calls=%async_computation.1 | async-start | bytes 8388608 | tf_op jit(solution)/shard_map/all_to_all | solution.py:272
  1541.0 8.9 slice-start.4
  1541.1 8.8 copy-start.61
  1541.1 8.9 slice-start.1
  1541.1 8.9 slice-start.5
  1596.1 7.3 copy-start.65
  1596.1 93.4 %all-to-all-start.3 = ((bf16[8,128,2048]{2,1,0:T(8,128)(2,1)}), bf16[8,128,2048]{2,1,0:T(8,128)(2,1)}, u32[]{:S(2)}, u32[]{:S(2)}) async-start(bf16[8,128,2048]{2,1,0:T(8,128)(2,1)} %bitcast.197), calls=%async_computation.3 | async-start | bytes 8388608 | tf_op jit(solution)/shard_map/all_to_all | solution.py:273
  1604.9 9.7 copy-start.62
  1604.9 9.7 copy-start.70
  1689.5 438.9 %copy-start.1 = (bf16[2048,512]{1,0:T(8,128)(2,1)S(1)}, bf16[2048,512]{1,0:T(8,128)(2,1)}, u32[]{:S(2)}) copy-start(bf16[2048,512]{1,0:T(8,128)(2,1)} %param.30) | copy-start | bytes 6291460
  (45 other events, 163.2 us)
Sparse Core Ops, SparseCore 0:
  206.9 290.9 all-reduce.13
  565.2 289.8 all-reduce.17
  857.5 153.9 all-reduce.15
  1186.6 292.6 all-reduce.19
  1482.4 32.3 reduce-scatter.30
  1518.5 60.9 reduce-scatter.14
  1583.7 69.8 reduce-scatter.12
  1657.5 50.4 reduce-scatter.22
  1712.3 51.3 reduce-scatter.18
  1767.4 51.2 reduce-scatter.16
  1822.6 33.3 reduce-scatter.20
  1859.9 86.8 reduce-scatter.28
  1950.9 86.7 reduce-scatter.26
  2041.6 86.7 reduce-scatter.24
where the time goes:
time: 2150 us; the launch traced here: 2140 us
  waiting for transfers between devices  1430 us (67%)
  matrix products  267 us (12%)
  local copies, waits for them, and re-layouts  168 us (8%)
  other arithmetic  159 us (7%)
  blocking collectives  73 us (3%)
    psum x1, waiting for transfers between devices, per_device(): d_feed = lax.psum(feed_part, 'tensor')  279 us
    psum x1, waiting for transfers between devices, per_device(): lax.psum((mixer_part, latent_part, d_head_gain, gain_term), 'tensor')  255 us
    psum x1, waiting for transfers between devices, per_device(): hidden = owner_rows + lax.psum(mixer_partial, 'tensor')  216 us
    psum x1, waiting for transfers between devices, per_device(): lax.psum(feed_partial.astype(jnp.bfloat16), 'tensor').astype(jnp.float32)  149 us
    reduce_scatter x1, waiting for transfers between devices, per_device(): lax.psum_scatter(grad_feed_up, 'dp', scatter_dimension=0, tiled=True)  90.9 us
    reduce_scatter x1, waiting for transfers between devices, per_device(): lax.psum_scatter(grad_feed_down, 'dp', scatter_dimension=0, tiled=True)  90.8 us
    reduce_scatter x1, waiting for transfers between devices, per_device(): lax.psum_scatter(grad_feed_gate, 'dp', scatter_dimension=0, tiled=True)  90.8 us
    dot_general x8, matrix products, contract_rows(): lax.dot_general(left_mat, right_mat, (((0,), (0,)), ((), ())), preferred_...  66.8 us
  transfers between devices with their start and end apart: 18, of which 14 were waited for; matrix products, arithmetic and copies ran while one was open for 10% of the time, Pallas kernels for 0%

commit v1 on v0

--- a/solution.py
+++ b/solution.py
@@ -200,7 +200,10 @@
     active = (swish_gate * up_hidden).astype(jnp.bfloat16)
     feed_partial = jnp.dot(active, feed_down, preferred_element_type=jnp.float32)
     layer_rows = (
-        hidden + lax.psum(feed_partial.astype(jnp.bfloat16), "tensor").astype(jnp.float32)
+        hidden
+        + jnp.sum(lax.all_gather(feed_partial.astype(jnp.bfloat16), "tensor"), axis=0).astype(
+            jnp.float32
+        )
     ).astype(jnp.bfloat16)
     upstream_wide = upstream.astype(jnp.float32)
     grad_feed_down = contract_rows(active, upstream)

time: 2150 us -> 2260 us (1.051)
  waiting for transfers between devices: 1430 us -> 1530 us
    all_gather x0 -> x1, waiting for transfers between devices: none -> 279 us  [per_device(): lax.all_gather(feed_partial.astype(jnp.bfloat16), 'tensor')]
    psum x1 -> x0, waiting for transfers between devices: 149 us -> none  [per_device(): lax.psum(feed_partial.astype(jnp.bfloat16), 'tensor').astype(jnp.float32)]
    reduce_scatter x1, waiting for transfers between devices: 90.8 us -> 3.76 us  [per_device(): lax.psum_scatter(grad_feed_down, 'dp', scatter_dimension=0, tiled=True)]
    psum x1, waiting for transfers between devices: 255 us -> 198 us  [per_device(): lax.psum((mixer_part, latent_part, d_head_gain, gain_term), 'tensor')]
    reduce_scatter x1, waiting for transfers between devices: 8.56 us -> 55.7 us  [per_device(): lax.psum_scatter(grad_out, 'dp', scatter_dimension=0, tiled=True)]
    reduce_scatter x1, waiting for transfers between devices: 0.01 us -> 45.4 us  [per_device(): lax.psum_scatter(grad_key, 'dp', scatter_dimension=0, tiled=True)]
    reduce_scatter x1, waiting for transfers between devices: 0.01 us -> 44.9 us  [per_device(): lax.psum_scatter(grad_query, 'dp', scatter_dimension=0, tiled=True)]
    all_to_all x1, waiting for transfers between devices: 26.1 us -> 0.01 us  [per_device(): lax.all_to_all(unplace_rows(layer_rows), 'dp', split_axis=0, concat_axis=...]
  transfers between devices with their start and end apart: 18 -> 18, of which waited for: 14 -> 15; matrix products, arithmetic and copies ran while one was open for 10% -> 9% of each run, Pallas kernels for 0% -> 0%
where the time goes in v1:
time: 2260 us; the launch traced here: 2240 us
  waiting for transfers between devices  1530 us (68%)
  matrix products  267 us (12%)
  other arithmetic  171 us (8%)
  local copies, waits for them, and re-layouts  167 us (7%)
  blocking collectives  69.9 us (3%)
    all_gather x1, waiting for transfers between devices, per_device(): lax.all_gather(feed_partial.astype(jnp.bfloat16), 'tensor')  279 us
    psum x1, waiting for transfers between devices, per_device(): d_feed = lax.psum(feed_part, 'tensor')  279 us
    psum x1, waiting for transfers between devices, per_device(): hidden = owner_rows + lax.psum(mixer_partial, 'tensor')  216 us
    psum x1, waiting for transfers between devices, per_device(): lax.psum((mixer_part, latent_part, d_head_gain, gain_term), 'tensor')  198 us
    reduce_scatter x1, waiting for transfers between devices, per_device(): lax.psum_scatter(grad_feed_up, 'dp', scatter_dimension=0, tiled=True)  91.3 us
    reduce_scatter x1, waiting for transfers between devices, per_device(): lax.psum_scatter(grad_feed_gate, 'dp', scatter_dimension=0, tiled=True)  91.3 us
    dot_general x8, matrix products, contract_rows(): lax.dot_general(left_mat, right_mat, (((0,), (0,)), ((), ())), preferred_...  67.1 us
    dot_general x8, matrix products, times_transposed(): lax.dot_general(left_mat, right_mat, (((1,), (1,)), ((), ())), preferred_...  64.4 us
  transfers between devices with their start and end apart: 18, of which 15 were waited for; matrix products, arithmetic and copies ran while one was open for 9% of the time, Pallas kernels for 0%

profile of v1, /device:TPU:0, one launch (start us, length us, event | category | flops | bytes accessed | tf_op | source)
XLA Modules:
  0.0 2241.7 jit_solution(4217456859577839967)
XLA Ops:
  11.7 10.5 scatter_custom_fusion.1
  22.2 5.3 all-to-all-start
  30.1 19.2 scatter_custom_fusion
  50.7 26.0 %all-to-all-done = bf16[8,128,2048]{2,1,0:T(8,128)(2,1)} async-done(((bf16[8,128,2048]{2,1,0:T(8,128)(2,1)}), bf16[8,128,2048]{2,1,0:T(8,128)(2,1)}, u32[]{:S(2)}, u32[]{:S(2)}) %all-to-all-start) | async-done | bytes 4194336 | tf_op jit(solution)/shard_map/all_to_all | solution.py:129
  76.7 10.2 scatter_custom_fusion.2
  109.1 6.7 fusion.66
  120.2 61.7 %while.36 = (s32[]{:T(128)}, f32[256,512]{1,0:T(8,128)S(1)}, f32[16,256,512]{2,1,0:T(8,128)}, f32[16,256]{1,0:T(8,128)S(1)}, f32[16,256,1]{1,2,0:T(1,128)}, /*in...) while((s32[]{:T(128)}, f32[256,512]{1,0:T(8,128)S(1)}, ...), condition=%wide.region_13.14_spmd.clone, body=%wide.region_12.13_spmd.clone.sunk | while | flops 524547 | bytes 2629268 | solution.py:62
  181.9 10.8 multiply_reduce_fusion.4
  192.9 6.9 multiply_convert_fusion.4
  200.8 5.6 fusion.85
  206.4 10.9 scatter_custom_fusion.3
  217.3 4.7 all-to-all-start.2
  222.1 49.1 %all-to-all-done.2 = bf16[8,128,2048]{2,1,0:T(8,128)(2,1)} async-done(((bf16[8,128,2048]{2,1,0:T(8,128)(2,1)}), bf16[8,128,2048]{2,1,0:T(8,128)(2,1)}, u32[]{:S(2)}, u32[]{:S(2)}) %all-to-all-start.2) | async-done | bytes 4194336 | tf_op jit(solution)/shard_map/all_to_all | solution.py:130
  271.1 10.1 scatter_custom_fusion.4
  281.3 216.3 %all-reduce.13.cloned.1.call-done = f32[1024,2048]{1,0:T(8,128)} async-done(((f32[1024,2048]{1,0:T(8,128)}), f32[1024,2048]{1,0:T(8,128)}) %all-reduce.13.cloned.1.call-update) | async-done | bytes 8388624 | tf_op jit(solution)/shard_map/psum | solution.py:193
  497.5 5.5 multiply_reduce_fusion.2
  506.3 11.8 fusion.87
  518.1 10.3 fusion.86
  528.5 15.1 multiply_convert_fusion.1
  543.6 9.7 fusion.88
  553.3 10.8 convolution_add_fusion.1
  564.2 10.9 convolution_convert_fusion
  575.2 279.0 %all-reduce.15.cloned.1.call-done = f32[1024,2048]{1,0:T(8,128)} async-done(((f32[1024,2048]{1,0:T(8,128)}), f32[1024,2048]{1,0:T(8,128)}) %all-reduce.15.cloned.1.call-update) | async-done | bytes 8388624 | tf_op jit(solution)/shard_map/psum | solution.py:218
  854.2 8.0 multiply_reduce_fusion
  862.2 279.4 %all-gather.3.cloned.1.call-done = bf16[4096,2048]{1,0:T(8,128)(2,1)} async-done(((bf16[1024,2048]{1,0:T(8,128)(2,1)}), bf16[4096,2048]{1,0:T(8,128)(2,1)}) %all-gather.3.cloned.1.call-update) | async-done | bytes 16777232 | tf_op jit(solution)/shard_map/all_gather | solution.py:204
  1141.6 12.1 reduce_sum.157
  1153.7 12.5 fusion.6
  1166.3 6.9 multiply_reduce_fusion.3
  1179.8 9.8 fusion.57
  1191.3 9.4 fusion.34
  1200.7 5.7 fusion.92
  1210.8 78.7 %while.37 = (s32[]{:T(128)}, f32[256,512]{1,0:T(8,128)S(1)}, f32[16,256,512]{2,1,0:T(8,128)}, f32[16,256]{1,0:T(8,128)S(1)}, f32[16,256,512]{2,1,0:T(8,128)}, /*...) while((s32[]{:T(128)}, f32[256,512]{1,0:T(8,128)S(1)}, ...), condition=%wide.region_25.26_spmd.clone, body=%wide.region_23.25_spmd.clone.sunk | while | flops 786692 | bytes 3157176 | solution.py:62
  1289.6 8.5 fusion.62
  1298.2 5.9 add_convert_fusion.1
  1311.7 5.7 fusion.91
  1319.7 9.1 add_add_fusion.2
  1332.3 11.8 fusion.12
  1344.2 12.1 fusion.99
  1356.4 11.9 fusion.98
  1368.3 4.9 fusion.94
  1373.4 4.9 fusion.93
  1378.3 8.0 fusion.24
  1387.5 6.8 fusion.96
  1394.4 4.9 concatenate.10
  1399.2 11.8 gather_fusion
  1411.1 4.7 all-to-all-start.1
  1415.8 6.7 fusion.95
  1422.5 198.4 %all-reduce.17.cloned.1.call-done = (f32[1024,2048]{1,0:T(8,128)}, f32[1024,16]{0,1:T(8,128)}) async-done(((f32[1024,2048]{1,0:T(8,128)}, f32[1024,16]{0,1:T(8,128)}), (f32[1024,2048]{1,0:T(8,128)}, f32[1024,16]{0,1:T(8,128)})) %all-reduce.17.cloned.1.call-update) | async-done | bytes 8454160 | tf_op jit(solution)/shard_map/psum | solution.py:241
  1620.9 9.0 fusion.5
  1633.7 4.7 concatenate.11
  1638.5 11.6 gather_fusion.2
  1650.1 4.7 all-to-all-start.3
  1663.6 9.7 gather_fusion.1
  1673.3 61.1 %all-reduce.7 = (f32[2048]{0:T(1024)S(1)}, f32[256]{0:T(256)S(1)}, f32[512]{0:T(512)S(1)}, f32[2048]{0:T(1024)S(1)}) all-reduce(f32[2048]{0:T(1024)S(1)} %get-tuple-element.304, f32[256]{0:T(256)S(1)} %neg.53, f32[512]{0:T(512)S(1)} %copy-done.74, f32[2048]{0:T(1024)S(1)} %copy-done.66), channel_id=3, replica_groups=mesh['dp'=8,'tensor'=4] {'dp'}, use_global_device_ids=true, to_apply=%region_32.33.clone | all-reduce | flops 4864 | bytes 38912
  1735.7 8.8 psum.40
  1745.2 9.9 gather_fusion.3
  1758.8 91.3 %reduce-scatter.27.cloned.1.call-done = f32[256,1408]{1,0:T(8,128)} async-done(((f32[2048,1408]{1,0:T(8,128)}), f32[256,1408]{1,0:T(8,128)}) %reduce-scatter.27.cloned.1.call-update) | async-done | bytes 1441808 | tf_op jit(solution)/shard_map/reduce_scatter | solution.py:271
  1850.0 91.3 %reduce-scatter.25.cloned.1.call-done = f32[256,1408]{1,0:T(8,128)} async-done(((f32[2048,1408]{1,0:T(8,128)}), f32[256,1408]{1,0:T(8,128)}) %reduce-scatter.25.cloned.1.call-update) | async-done | bytes 1441808 | tf_op jit(solution)/shard_map/reduce_scatter | solution.py:270
  1941.3 45.4 %reduce-scatter.15.cloned.1.call-done = f32[256,256]{1,0:T(8,128)} async-done(((f32[2048,256]{1,0:T(8,128)}), f32[256,256]{1,0:T(8,128)}) %reduce-scatter.15.cloned.1.call-update) | async-done | bytes 262160 | tf_op jit(solution)/shard_map/reduce_scatter | solution.py:261
  1986.8 44.9 %reduce-scatter.13.cloned.1.call-done = f32[256,256]{1,0:T(8,128)} async-done(((f32[2048,256]{1,0:T(8,128)}), f32[256,256]{1,0:T(8,128)}) %reduce-scatter.13.cloned.1.call-update) | async-done | bytes 262160 | tf_op jit(solution)/shard_map/reduce_scatter | solution.py:260
  2031.7 55.7 %reduce-scatter.23.cloned.1.call-done = f32[64,2048]{1,0:T(8,128)} async-done(((f32[512,2048]{1,0:T(8,128)}), f32[64,2048]{1,0:T(8,128)}) %reduce-scatter.23.cloned.1.call-update) | async-done | bytes 524304 | tf_op jit(solution)/shard_map/reduce_scatter | solution.py:268
  2087.4 55.1 %reduce-scatter.19.cloned.1.call-done = f32[256,512]{1,0:T(8,128)} async-done(((f32[2048,512]{1,0:T(8,128)}), f32[256,512]{1,0:T(8,128)}) %reduce-scatter.19.cloned.1.call-update) | async-done | bytes 524304 | tf_op jit(solution)/shard_map/reduce_scatter | solution.py:263
  2142.5 55.7 %reduce-scatter.17.cloned.1.call-done = f32[256,512]{1,0:T(8,128)} async-done(((f32[2048,512]{1,0:T(8,128)}), f32[256,512]{1,0:T(8,128)}) %reduce-scatter.17.cloned.1.call-update) | async-done | bytes 524304 | tf_op jit(solution)/shard_map/reduce_scatter | solution.py:262
  2198.2 36.8 %reduce-scatter.21.cloned.1.call-done = f32[256,16]{0,1:T(8,128)} async-done(((f32[2048,16]{0,1:T(8,128)}), f32[256,16]{0,1:T(8,128)}) %reduce-scatter.21.cloned.1.call-update) | async-done | bytes 16400 | tf_op jit(solution)/shard_map/reduce_scatter | solution.py:264
  (509 shorter events, 221.9 us)
Async XLA Ops:
  7.2 185.7 %copy-start = (bf16[2048,512]{1,0:T(8,128)(2,1)S(1)}, bf16[2048,512]{1,0:T(8,128)(2,1)}, u32[]{:S(2)}) copy-start(bf16[2048,512]{1,0:T(8,128)(2,1)} %param.30) | copy-start | bytes 6291460
  11.7 194.7 %copy-start.68 = (s32[640]{0:T(1024)}, s32[640]{0:T(1024)S(1)}, u32[]{:S(2)}) copy-start(s32[640]{0:T(1024)S(1)} %compare_select_fusion.4) | copy-start | bytes 7684
  22.2 54.5 %all-to-all-start = ((bf16[8,128,2048]{2,1,0:T(8,128)(2,1)}), bf16[8,128,2048]{2,1,0:T(8,128)(2,1)}, u32[]{:S(2)}, u32[]{:S(2)}) async-start(bf16[8,128,2048]{2,1,0:T(8,128)(2,1)} %bitcast.201), calls=%async_computation | async-start | bytes 8388608 | tf_op jit(solution)/shard_map/all_to_all | solution.py:129
  27.5 470.0 %all-reduce.13.cloned.1.call-start = ((), (), s32[]{:S(2)}) async-start(), calls=%async_computation.14 | async-start | bytes 16777216 | tf_op jit(solution)/shard_map/psum | solution.py:193
  27.9 76.1 %copy-start.41 = (s32[16,64]{1,0:T(8,128)}, s32[16,64]{1,0:T(8,128)S(1)}, u32[]{:S(2)}) copy-start(s32[16,64]{1,0:T(8,128)S(1)} %eq.92) | copy-start | bytes 12292
  28.0 62.1 %copy-start.53 = (f32[2048]{0:T(1024)}, f32[2048]{0:T(1024)S(1)}, u32[]{:S(2)}) copy-start(f32[2048]{0:T(1024)S(1)} %convert_element_type.129) | copy-start | bytes 24580
  49.7 54.4 %copy-start.57 = (pred[64,64]{1,0:T(8,128)(4,1)}, pred[64,64]{1,0:T(8,128)(4,1)S(1)}, u32[]{:S(2)}) copy-start(pred[64,64]{1,0:T(8,128)(4,1)S(1)} %iota_compare_fusion) | copy-start | bytes 12292
  49.9 59.2 %copy-start.55 = (f32[16,64]{1,0:T(8,128)}, f32[16,64]{1,0:T(8,128)S(1)}, u32[]{:S(2)}) copy-start(f32[16,64]{1,0:T(8,128)S(1)} %get-tuple-element.369) | copy-start | bytes 12292
  49.9 132.0 %copy-start.50 = (f32[16,64]{1,0:T(8,128)}, f32[16,64]{1,0:T(8,128)S(1)}, u32[]{:S(2)}) copy-start(f32[16,64]{1,0:T(8,128)S(1)} %get-tuple-element.370) | copy-start | bytes 12292
  96.8 12.3 copy-start.12
  99.2 9.9 copy-start.15
  106.8 9.0 copy-start.19
  181.9 10.9 copy-start.43
  181.9 10.9 copy-start.67
  181.9 10.9 copy-start.76
  192.9 7.9 copy-start.78
  217.3 53.8 %all-to-all-start.2 = ((bf16[8,128,2048]{2,1,0:T(8,128)(2,1)}), bf16[8,128,2048]{2,1,0:T(8,128)(2,1)}, u32[]{:S(2)}, u32[]{:S(2)}) async-start(bf16[8,128,2048]{2,1,0:T(8,128)(2,1)} %bitcast.202), calls=%async_computation.2 | async-start | bytes 8388608 | tf_op jit(solution)/shard_map/all_to_all | solution.py:130
  222.0 632.2 %all-reduce.15.cloned.1.call-start = ((), (), s32[]{:S(2)}) async-start(), calls=%async_computation.15 | async-start | bytes 16777216 | tf_op jit(solution)/shard_map/psum | solution.py:218
  506.3 11.8 copy-start.23
  506.3 22.1 slice-start.6
  518.1 10.3 slice-start.7
  543.6 9.8 copy-start.84
  564.2 577.4 %all-gather.3.cloned.1.call-start = ((), (), s32[]{:S(2)}) async-start(), calls=%async_computation.25 | async-start | bytes 20971520 | tf_op jit(solution)/shard_map/all_gather | solution.py:204
  575.2 1045.7 %all-reduce.17.cloned.1.call-start = ((), (), s32[]{:S(2)}) async-start(), calls=%async_computation.27 | async-start | bytes 16908288 | tf_op jit(solution)/shard_map/psum | solution.py:241
  1153.7 12.5 copy-start.18
  1153.7 12.5 copy-start.30
  1175.2 25.5 %copy-start.34 = (bf16[1024,512]{1,0:T(8,128)(2,1)}, bf16[1024,512]{1,0:T(8,128)(2,1)S(1)}, u32[]{:S(2)}) copy-start(bf16[1024,512]{1,0:T(8,128)(2,1)S(1)} %get-tuple-element.363) | copy-start | bytes 3145732
  1175.2 16.1 slice-start.2
  1176.4 13.2 copy-start.21
  1179.8 9.8 copy-start.6
  1179.8 9.8 copy-start.13
  1179.8 11.5 slice-start.3
  1210.8 78.8 %copy-start.14 = (bf16[1024,256]{1,0:T(8,128)(2,1)S(1)}, bf16[1024,256]{1,0:T(8,128)(2,1)}, u32[]{:S(2)}) copy-start(bf16[1024,256]{1,0:T(8,128)(2,1)} %copy-done.12) | copy-start | bytes 1572868
  1210.8 78.8 %copy-start.44 = (f32[16,256]{1,0:T(8,128)S(1)}, f32[16,256]{1,0:T(8,128)}, u32[]{:S(2)}) copy-start(f32[16,256]{1,0:T(8,128)} %copy-done.43) | copy-start | bytes 49156
  1210.8 78.8 %copy-start.56 = (f32[16,64]{1,0:T(8,128)S(1)}, f32[16,64]{1,0:T(8,128)}, u32[]{:S(2)}) copy-start(f32[16,64]{1,0:T(8,128)} %copy-done.55) | copy-start | bytes 12292
  1289.6 8.6 copy-start.3
  1289.6 8.6 copy-start.17
  1304.1 7.6 copy-start.39
  1307.2 10.2 copy-start.27
  1328.9 333.3 %reduce-scatter.31.cloned.1.call-start = ((), (), s32[]{:S(2)}) async-start(), calls=%async_computation.26 | async-start | bytes 147456
  1332.2 426.6 %reduce-scatter.29.cloned.1.call-start = ((), (), s32[]{:S(2)}) async-start(), calls=%async_computation.24 | async-start | bytes 12976128 | tf_op jit(solution)/shard_map/reduce_scatter | solution.py:272
  1344.1 505.9 %reduce-scatter.27.cloned.1.call-start = ((), (), s32[]{:S(2)}) async-start(), calls=%async_computation.23 | async-start | bytes 12976128 | tf_op jit(solution)/shard_map/reduce_scatter | solution.py:271
  1356.4 585.0 %reduce-scatter.25.cloned.1.call-start = ((), (), s32[]{:S(2)}) async-start(), calls=%async_computation.22 | async-start | bytes 12976128 | tf_op jit(solution)/shard_map/reduce_scatter | solution.py:270
  1368.3 618.5 %reduce-scatter.15.cloned.1.call-start = ((), (), s32[]{:S(2)}) async-start(), calls=%async_computation.17 | async-start | bytes 2359296 | tf_op jit(solution)/shard_map/reduce_scatter | solution.py:261
  1373.3 658.4 %reduce-scatter.13.cloned.1.call-start = ((), (), s32[]{:S(2)}) async-start(), calls=%async_computation.16 | async-start | bytes 2359296 | tf_op jit(solution)/shard_map/reduce_scatter | solution.py:260
  1378.3 709.1 %reduce-scatter.23.cloned.1.call-start = ((), (), s32[]{:S(2)}) async-start(), calls=%async_computation.21 | async-start | bytes 4718592 | tf_op jit(solution)/shard_map/reduce_scatter | solution.py:268
  1386.3 756.2 %reduce-scatter.19.cloned.1.call-start = ((), (), s32[]{:S(2)}) async-start(), calls=%async_computation.19 | async-start | bytes 4718592 | tf_op jit(solution)/shard_map/reduce_scatter | solution.py:263
  1411.1 239.0 %all-to-all-start.1 = ((bf16[8,128,2048]{2,1,0:T(8,128)(2,1)}), bf16[8,128,2048]{2,1,0:T(8,128)(2,1)}, u32[]{:S(2)}, u32[]{:S(2)}) async-start(bf16[8,128,2048]{2,1,0:T(8,128)(2,1)} %bitcast.199), calls=%async_computation.1 | async-start | bytes 8388608 | tf_op jit(solution)/shard_map/all_to_all | solution.py:275
  1415.8 782.4 %reduce-scatter.17.cloned.1.call-start = ((), (), s32[]{:S(2)}) async-start(), calls=%async_computation.18 | async-start | bytes 4718592 | tf_op jit(solution)/shard_map/reduce_scatter | solution.py:262
  1415.8 214.1 %slice-start = ((s8[4227072]{0:T(1024)(128)(4,1)}), s8[32768]{0:T(1024)(128)(4,1)S(1)}, s32[]{:S(2)}) async-start(s8[4227072]{0:T(1024)(128)(4,1)} %bitcast.177), calls=%async_computation.28 | async-start | bytes 65536
  1422.5 198.4 %copy-start.48 = (bf16[2048,16]{0,1:T(8,128)(2,1)S(1)}, bf16[2048,16]{0,1:T(8,128)(2,1)}, u32[]{:S(2)}) copy-start(bf16[2048,16]{0,1:T(8,128)(2,1)} %param.31) | copy-start | bytes 196612
  1422.5 198.4 %copy-start.54 = (f32[2048]{0:T(1024)S(1)}, f32[2048]{0:T(1024)}, u32[]{:S(2)}) copy-start(f32[2048]{0:T(1024)} %copy-done.53) | copy-start | bytes 24580
  1422.5 198.4 %copy-start.60 = (f32[1024]{0:T(1024)S(1)}, f32[1024]{0:T(1024)}, u32[]{:S(2)}) copy-start(f32[1024]{0:T(1024)} %copy-done.59) | copy-start | bytes 12292
  1620.9 9.1 slice-start.4
  1620.9 9.0 copy-start.63
  1620.9 9.1 slice-start.1
  1620.9 9.1 slice-start.5
  1650.1 7.5 copy-start.49
  1650.1 95.1 %all-to-all-start.3 = ((bf16[8,128,2048]{2,1,0:T(8,128)(2,1)}), bf16[8,128,2048]{2,1,0:T(8,128)(2,1)}, u32[]{:S(2)}, u32[]{:S(2)}) async-start(bf16[8,128,2048]{2,1,0:T(8,128)(2,1)} %bitcast.198), calls=%async_computation.3 | async-start | bytes 8388608 | tf_op jit(solution)/shard_map/all_to_all | solution.py:276
  1654.8 7.4 copy-start.69
  1654.8 580.2 %reduce-scatter.21.cloned.1.call-start = ((), (), s32[]{:S(2)}) async-start(), calls=%async_computation.20 | async-start | bytes 147456 | tf_op jit(solution)/shard_map/reduce_scatter | solution.py:264
  1663.6 9.7 copy-start.66
  1663.6 9.7 copy-start.74
  1745.2 489.8 %copy-start.1 = (bf16[2048,512]{1,0:T(8,128)(2,1)S(1)}, bf16[2048,512]{1,0:T(8,128)(2,1)}, u32[]{:S(2)}) copy-start(bf16[2048,512]{1,0:T(8,128)(2,1)} %param.30) | copy-start | bytes 6291460
  (49 other events, 201.3 us)
Sparse Core Ops, SparseCore 0:
  206.5 290.9 all-reduce.12
  564.3 289.8 all-reduce.14
  855.8 285.7 all-gather.2
  1329.0 291.8 all-reduce.16
  1623.7 32.3 reduce-scatter.30
  1660.5 98.2 reduce-scatter.28
  1763.3 86.7 reduce-scatter.26
  1854.5 86.7 reduce-scatter.24
  1945.5 41.1 reduce-scatter.14
  1990.5 41.1 reduce-scatter.12
  2036.0 51.3 reduce-scatter.22
  2091.2 51.2 reduce-scatter.18
  2146.8 51.3 reduce-scatter.16
  2201.6 33.3 reduce-scatter.20
